TPU v7x, 32 devices: a whole 2x2x4 slice. The times are simulated.
32 devices in a mesh: ctx: 8 (over y, x, core), tp: 4 (over z).
Axes of the slice: x: 2, y: 2, z: 4, core: 2. Of those that a mesh axis runs over, the one named last changes fastest.
Arguments:
- tokens: bfloat16 [4096, 2048], P('ctx'), may hold values from -6 to 6
- cotangent: bfloat16 [4096, 2048], P('ctx'), may hold values from -6 to 6
- w_qkv: float32 [3, 2048, 2048], P(None, 'ctx', 'tp'), may hold values from -0.125 to 0.125
- w_out: float32 [2048, 2048], P('tp', 'ctx'), may hold values from -0.75 to 0.75
- w_up: float32 [2048, 8192], P('ctx', 'tp'), may hold values from -0.125 to 0.125
- w_down: float32 [8192, 2048], P('tp', 'ctx'), may hold values from -0.0625 to 0.0625
- norm_gains: float32 [2, 2048], P(None, 'ctx'), may hold values from 0.25 to 1.75
- norm_biases: float32 [2, 2048], P(None, 'ctx'), may hold values from -3 to 3
- m_qkv: float32 [3, 2048, 2048], P(None, 'ctx', 'tp'), may hold values from -0.00024414062 to 0.00024414062
- m_out: float32 [2048, 2048], P('tp', 'ctx'), may hold values from -0.00024414062 to 0.00024414062
- m_up: float32 [2048, 8192], P('ctx', 'tp'), may hold values from -0.00024414062 to 0.00024414062
- m_down: float32 [8192, 2048], P('tp', 'ctx'), may hold values from -0.00024414062 to 0.00024414062
- m_gains: float32 [2, 2048], P(None, 'ctx'), may hold values from -0.00024414062 to 0.00024414062
- m_biases: float32 [2, 2048], P(None, 'ctx'), may hold values from -0.00024414062 to 0.00024414062
- v_qkv: float32 [3, 2048, 2048], P(None, 'ctx', 'tp'), may hold values from 3.9729964e-10 to 3.9729965e-08
- v_out: float32 [2048, 2048], P('tp', 'ctx'), may hold values from 3.9729964e-10 to 3.9729965e-08
- v_up: float32 [2048, 8192], P('ctx', 'tp'), may hold values from 3.9729964e-10 to 3.9729965e-08
- v_down: float32 [8192, 2048], P('tp', 'ctx'), may hold values from 3.9729964e-10 to 3.9729965e-08
- v_gains: float32 [2, 2048], P(None, 'ctx'), may hold values from 3.9729964e-10 to 3.9729965e-08
- v_biases: float32 [2, 2048], P(None, 'ctx'), may hold values from 3.9729964e-10 to 3.9729965e-08
- seq_lengths: int32 [4], replicated, may hold values from 1 to 2048, 4096 in all
- decay_mask: int32 [6], replicated, may hold values 0 or 1
Outputs:
- block_out: bfloat16 [4096, 2048], P('ctx')
- grad_tokens: bfloat16 [4096, 2048], P('ctx')
- grad_norm: float32 [], replicated
- grad_qkv: float32 [3, 2048, 2048], P(None, 'ctx', 'tp')
- grad_out: float32 [2048, 2048], P('tp', 'ctx')
- grad_up: float32 [2048, 8192], P('ctx', 'tp')
- grad_down: float32 [8192, 2048], P('tp', 'ctx')
- grad_gains: float32 [2, 2048], P(None, 'ctx')
- grad_biases: float32 [2, 2048], P(None, 'ctx')
- step_qkv: float32 [3, 2048, 2048], P(None, 'ctx', 'tp')
- step_out: float32 [2048, 2048], P('tp', 'ctx')
- step_up: float32 [2048, 8192], P('ctx', 'tp')
- step_down: float32 [8192, 2048], P('tp', 'ctx')
- step_gains: float32 [2, 2048], P(None, 'ctx')
- step_biases: float32 [2, 2048], P(None, 'ctx')
- first_qkv: float32 [3, 2048, 2048], P(None, 'ctx', 'tp')
- first_out: float32 [2048, 2048], P('tp', 'ctx')
- first_up: float32 [2048, 8192], P('ctx', 'tp')
- first_down: float32 [8192, 2048], P('tp', 'ctx')
- first_gains: float32 [2, 2048], P(None, 'ctx')
- first_biases: float32 [2, 2048], P(None, 'ctx')
- second_qkv: float32 [3, 2048, 2048], P(None, 'ctx', 'tp')
- second_out: float32 [2048, 2048], P('tp', 'ctx')
- second_up: float32 [2048, 8192], P('ctx', 'tp')
- second_down: float32 [8192, 2048], P('tp', 'ctx')
- second_gains: float32 [2, 2048], P(None, 'ctx')
- second_biases: float32 [2, 2048], P(None, 'ctx')
Inputs may be any that keep to these rules, and one draw needn't show every extreme that they name: `seq_lengths`: the lengths sum to 4096.
All inputs are finite; a program needn't handle non-finite values.
Results may differ from a plain program's by a relative error of at most 0.012.
Values may be sent and summed in bfloat16 or wider, within the bound.
No kernel may reach another device: no remote copies, remote signals or barrier semaphores. Data moves between devices by JAX's collectives and lax.ppermute only.
A program may use at most 256 MiB of HBM per device.

v0:
```python
import math
import jax
import jax.numpy as jnp
from jax import lax
from jax.sharding import PartitionSpec as P

D = 2048
HEADS = 16
SEQ_MAX = 2048
BLOCK = 256
eps_norm = 1e-05
neg_big = -1e30
beta_one = 0.9
beta_two = 0.95
adam_eps = 1e-08
learn_rate = 0.001
decay_rate = 0.1
step_count = 10.0
inv_root_two = 1.0 / math.sqrt(2.0)
inv_root_two_pi = 1.0 / math.sqrt(2.0 * math.pi)


def passed_along(value, axis, steps):
    count = lax.axis_size(axis)
    first, last = (max(0, -steps), min(count, count - steps))
    return lax.ppermute(value, axis, [(source, source + steps) for source in range(first, last)])


def token_labels(global_rows, seq_lengths, total_rows):
    starts = jnp.cumsum(seq_lengths) - seq_lengths
    after = (global_rows[:, None] >= starts[None, :]).astype(jnp.int32)
    segment = jnp.sum(after, axis=1) - 1
    chosen = segment[:, None] == jnp.arange(seq_lengths.shape[0], dtype=jnp.int32)[None, :]
    begin = jnp.sum(jnp.where(chosen, starts[None, :], 0), axis=1)
    block = (global_rows - begin) // BLOCK
    valid = (global_rows >= 0) & (global_rows < total_rows)
    return (segment, block, valid)


def layer_norm(rows, gain, bias):
    mean = jnp.mean(rows, axis=1, keepdims=True)
    centred = rows - mean
    rstd = lax.rsqrt(jnp.mean(centred * centred, axis=1, keepdims=True) + eps_norm)
    normed = centred * rstd
    return (normed * gain + bias, normed, rstd)


def norm_back(grad_out, normed, rstd, gain):
    scaled = grad_out * gain
    inner = (
        scaled
        - jnp.mean(scaled, axis=1, keepdims=True)
        - normed * jnp.mean(scaled * normed, axis=1, keepdims=True)
    )
    return (inner * rstd, jnp.sum(grad_out * normed, axis=0), jnp.sum(grad_out, axis=0))


def gelu_slope(values):
    return (
        0.5 * (1.0 + lax.erf(values * inv_root_two))
        + values * jnp.exp(-0.5 * values * values) * inv_root_two_pi
    )


def split_heads(values, head_size):
    return values.reshape(values.shape[0], -1, head_size)


def attention_probs(query, keys, allowed, scale, lse_kept):
    raw = jnp.einsum("qhd,khd->hqk", query, keys, preferred_element_type=jnp.float32) * scale
    masked = jnp.where(allowed[None], raw, neg_big)
    if lse_kept is None:
        top = jnp.max(masked, axis=2, keepdims=True)
        lse = top + jnp.log(jnp.sum(jnp.exp(masked - top), axis=2, keepdims=True))
    else:
        lse = lse_kept
    return (jnp.exp(masked - lse), lse)


def adam_update(master, grad, first, second, factor, decays):
    clipped = grad * factor
    first_new = beta_one * first + (1.0 - beta_one) * clipped
    second_new = beta_two * second + (1.0 - beta_two) * clipped * clipped
    fix_one = 1.0 - beta_one**step_count
    fix_two = 1.0 - beta_two**step_count
    update = first_new / fix_one / (jnp.sqrt(second_new / fix_two) + adam_eps)
    amount = learn_rate * (update + decay_rate * decays * master)
    return (amount, first_new, second_new)


def per_device(
    tokens,
    cotangent,
    w_qkv,
    w_out,
    w_up,
    w_down,
    norm_gains,
    norm_biases,
    m_qkv,
    m_out,
    m_up,
    m_down,
    m_gains,
    m_biases,
    v_qkv,
    v_out,
    v_up,
    v_down,
    v_gains,
    v_biases,
    seq_lengths,
    decay_mask,
):
    rows = tokens.shape[0]
    ctx_count = lax.axis_size("ctx")
    ctx_place = lax.axis_index("ctx")
    tp_place = lax.axis_index("tp")
    total_rows = rows * ctx_count
    head_size = D // HEADS
    scale = head_size ** (-0.5)
    reach = SEQ_MAX // rows
    offsets = [-1] + list(range(1, reach + 1))
    local_rows = jnp.arange(rows, dtype=jnp.int32)
    full = (
        lax.all_gather(w_qkv.astype(jnp.bfloat16), "ctx", axis=1, tiled=True),
        lax.all_gather(w_out.astype(jnp.bfloat16), "ctx", axis=1, tiled=True),
        lax.all_gather(w_up.astype(jnp.bfloat16), "ctx", axis=0, tiled=True),
        lax.all_gather(w_down.astype(jnp.bfloat16), "ctx", axis=1, tiled=True),
        lax.all_gather(norm_gains.astype(jnp.bfloat16), "ctx", axis=1, tiled=True),
        lax.all_gather(norm_biases.astype(jnp.bfloat16), "ctx", axis=1, tiled=True),
    )
    qkv_full, out_full, up_full, down_full, gains_full, biases_full = full
    gains32 = gains_full.astype(jnp.float32)
    biases32 = biases_full.astype(jnp.float32)
    x32 = tokens.astype(jnp.float32)
    h1, normed1, rstd1 = layer_norm(x32, gains32[0], biases32[0])
    a1 = h1.astype(jnp.bfloat16)
    qkv = jnp.einsum("td,cdh->cth", a1, qkv_full, preferred_element_type=jnp.float32).astype(
        jnp.bfloat16
    )
    query = qkv[0]
    kv_own = qkv[1:]
    own_rows = ctx_place * rows + local_rows
    key_rows = [own_rows]
    for offset in offsets:
        key_rows.append((ctx_place - offset) * rows + local_rows)
    key_rows = jnp.concatenate(key_rows)
    q_seg, q_blk, _ = token_labels(own_rows, seq_lengths, total_rows)
    k_seg, k_blk, k_valid = token_labels(key_rows, seq_lengths, total_rows)
    allowed = (
        k_valid[None, :] & (k_seg[None, :] == q_seg[:, None]) & (k_blk[None, :] <= q_blk[:, None])
    )
    pieces = [kv_own]
    for offset in offsets:
        pieces.append(passed_along(kv_own, "ctx", offset))
    kv_all = jnp.concatenate(pieces, axis=1)
    q3 = split_heads(query, head_size)
    k3 = split_heads(kv_all[0], head_size)
    v3 = split_heads(kv_all[1], head_size)
    prob, lse = attention_probs(q3, k3, allowed, scale, None)
    prob_low = prob.astype(jnp.bfloat16)
    attn_vals = jnp.einsum("hqk,khd->qhd", prob_low, v3, preferred_element_type=jnp.float32)
    attn_vals = attn_vals.reshape(rows, -1).astype(jnp.bfloat16)
    attn = lax.psum(jnp.dot(attn_vals, out_full, preferred_element_type=jnp.float32), "tp")
    y1 = x32 + attn
    h2, normed2, rstd2 = layer_norm(y1, gains32[1], biases32[1])
    a2 = h2.astype(jnp.bfloat16)
    up = jnp.dot(a2, up_full, preferred_element_type=jnp.float32)
    act_low = jax.nn.gelu(up, approximate=False).astype(jnp.bfloat16)
    mixed = lax.psum(
        jnp.dot(act_low, down_full, preferred_element_type=jnp.float32).astype(jnp.bfloat16), "tp"
    ).astype(jnp.float32)
    block_out = (y1 + mixed).astype(jnp.bfloat16)
    grad_down = jnp.dot(act_low.T, cotangent, preferred_element_type=jnp.float32)
    grad_act = jnp.dot(cotangent, down_full.T, preferred_element_type=jnp.float32)
    grad_up_in = (grad_act * gelu_slope(up)).astype(jnp.bfloat16)
    grad_up = jnp.dot(a2.T, grad_up_in, preferred_element_type=jnp.float32)
    grad_h2 = lax.psum(jnp.dot(grad_up_in, up_full.T, preferred_element_type=jnp.float32), "tp")
    grad_y1_norm, gain_two, bias_two = norm_back(grad_h2, normed2, rstd2, gains32[1])
    grad_y1 = cotangent.astype(jnp.float32) + grad_y1_norm
    grad_attn = grad_y1.astype(jnp.bfloat16)
    grad_outw = jnp.dot(attn_vals.T, grad_attn, preferred_element_type=jnp.float32)
    grad_vals = jnp.dot(grad_attn, out_full.T, preferred_element_type=jnp.float32).astype(
        jnp.bfloat16
    )
    prob, _ = attention_probs(q3, k3, allowed, scale, lse)
    prob_low = prob.astype(jnp.bfloat16)
    g3 = split_heads(grad_vals, head_size)
    grad_prob = jnp.einsum("qhd,khd->hqk", g3, v3, preferred_element_type=jnp.float32)
    inner = jnp.sum(prob * grad_prob, axis=2, keepdims=True)
    grad_scores = (prob * (grad_prob - inner)).astype(jnp.bfloat16)
    grad_query = (
        jnp.einsum("hqk,khd->qhd", grad_scores, k3, preferred_element_type=jnp.float32) * scale
    )
    grad_keys = (
        jnp.einsum("hqk,qhd->khd", grad_scores, q3, preferred_element_type=jnp.float32) * scale
    )
    grad_values = jnp.einsum("hqk,qhd->khd", prob_low, g3, preferred_element_type=jnp.float32)
    kv_grad = jnp.stack(
        (grad_keys.reshape(grad_keys.shape[0], -1), grad_values.reshape(grad_values.shape[0], -1))
    )
    kv_total = kv_grad[:, :rows]
    for place, offset in enumerate(offsets):
        piece = kv_grad[:, (place + 1) * rows : (place + 2) * rows]
        kv_total = kv_total + passed_along(piece, "ctx", -offset)
    grad_qkv_in = jnp.concatenate((grad_query.reshape(rows, -1)[None], kv_total), axis=0).astype(
        jnp.bfloat16
    )
    grad_qkvw = jnp.einsum("td,cth->cdh", a1, grad_qkv_in, preferred_element_type=jnp.float32)
    part_one = jnp.einsum("cth,cdh->td", grad_qkv_in, qkv_full, preferred_element_type=jnp.float32)
    grad_h1 = lax.psum(part_one, "tp")
    grad_x_norm, gain_one, bias_one = norm_back(grad_h1, normed1, rstd1, gains32[0])
    grad_tokens = (grad_y1 + grad_x_norm).astype(jnp.bfloat16)
    grad_gainw = jnp.stack((gain_one, gain_two))
    grad_biasw = jnp.stack((bias_one, bias_two))
    shards = (
        lax.psum_scatter(grad_qkvw, "ctx", scatter_dimension=1, tiled=True),
        lax.psum_scatter(grad_outw, "ctx", scatter_dimension=1, tiled=True),
        lax.psum_scatter(grad_up, "ctx", scatter_dimension=0, tiled=True),
        lax.psum_scatter(grad_down, "ctx", scatter_dimension=1, tiled=True),
        lax.psum_scatter(grad_gainw, "ctx", scatter_dimension=1, tiled=True),
        lax.psum_scatter(grad_biasw, "ctx", scatter_dimension=1, tiled=True),
    )
    matrix_sq = jnp.sum(shards[0] * shards[0]) + jnp.sum(shards[1] * shards[1])
    matrix_sq = matrix_sq + jnp.sum(shards[2] * shards[2]) + jnp.sum(shards[3] * shards[3])
    small_sq = jnp.sum(shards[4] * shards[4]) + jnp.sum(shards[5] * shards[5])
    local_sq = matrix_sq + jnp.where(tp_place == 0, small_sq, jnp.float32(0.0))
    total_sq = lax.psum(local_sq, ("ctx", "tp"))
    grad_norm = jnp.sqrt(total_sq)
    factor = 1.0 / jnp.maximum(grad_norm, 1.0)
    masters = (w_qkv, w_out, w_up, w_down, norm_gains, norm_biases)
    firsts = (m_qkv, m_out, m_up, m_down, m_gains, m_biases)
    seconds = (v_qkv, v_out, v_up, v_down, v_gains, v_biases)
    amounts, new_first, new_second = ([], [], [])
    for place in range(6):
        decays = decay_mask[place].astype(jnp.float32)
        amount, first_new, second_new = adam_update(
            masters[place], shards[place], firsts[place], seconds[place], factor, decays
        )
        amounts.append(amount)
        new_first.append(first_new)
        new_second.append(second_new)
    return (
        block_out,
        grad_tokens,
        grad_norm,
        shards[0],
        shards[1],
        shards[2],
        shards[3],
        shards[4],
        shards[5],
        amounts[0],
        amounts[1],
        amounts[2],
        amounts[3],
        amounts[4],
        amounts[5],
        new_first[0],
        new_first[1],
        new_first[2],
        new_first[3],
        new_first[4],
        new_first[5],
        new_second[0],
        new_second[1],
        new_second[2],
        new_second[3],
        new_second[4],
        new_second[5],
    )


def solution(mesh):
    return jax.shard_map(
        per_device,
        mesh=mesh,
        in_specs=(
            P("ctx", None),
            P("ctx", None),
            P(None, "ctx", "tp"),
            P("tp", "ctx"),
            P("ctx", "tp"),
            P("tp", "ctx"),
            P(None, "ctx"),
            P(None, "ctx"),
            P(None, "ctx", "tp"),
            P("tp", "ctx"),
            P("ctx", "tp"),
            P("tp", "ctx"),
            P(None, "ctx"),
            P(None, "ctx"),
            P(None, "ctx", "tp"),
            P("tp", "ctx"),
            P("ctx", "tp"),
            P("tp", "ctx"),
            P(None, "ctx"),
            P(None, "ctx"),
            P(),
            P(),
        ),
        out_specs=(
            P("ctx", None),
            P("ctx", None),
            P(),
            P(None, "ctx", "tp"),
            P("tp", "ctx"),
            P("ctx", "tp"),
            P("tp", "ctx"),
            P(None, "ctx"),
            P(None, "ctx"),
            P(None, "ctx", "tp"),
            P("tp", "ctx"),
            P("ctx", "tp"),
            P("tp", "ctx"),
            P(None, "ctx"),
            P(None, "ctx"),
            P(None, "ctx", "tp"),
            P("tp", "ctx"),
            P("ctx", "tp"),
            P("tp", "ctx"),
            P(None, "ctx"),
            P(None, "ctx"),
            P(None, "ctx", "tp"),
            P("tp", "ctx"),
            P("ctx", "tp"),
            P("tp", "ctx"),
            P(None, "ctx"),
            P(None, "ctx"),
        ),
        check_vma=False,
    )
```

profile of v0, /device:TPU:0, one launch (start us, length us, event | category | flops | bytes accessed | tf_op | source)
XLA Modules:
  0.0 1714.8 jit_solution(7258916373576961367)
XLA Ops:
  7.3 3.2 copy.83
  13.8 10.3 all_gather.19
  24.2 8.9 all_gather.18
  34.8 27.6 %all-gather.5.cloned.1.call-done = bf16[3,2048,512]{1,2,0:T(8,128)(2,1)} async-done(((bf16[3,256,512]{1,2,0:T(8,128)(2,1)}), bf16[3,2048,512]{1,2,0:T(8,128)(2,1)}) %all-gather.5.cloned.1.call-update) | async-done | bytes 6291472 | tf_op jit(solution)/shard_map/all_gather | solution.py:126
  62.5 6.6 fusion.48
  70.7 3.1 collective-permute-start.1
  73.8 3.4 collective-permute-start.2
  77.2 3.9 collective-permute-start.3
  85.3 21.0 %collective-permute-done.2 = bf16[2,512,512]{1,2,0:T(8,128)(2,1)S(1)} collective-permute-done((bf16[2,512,512]{1,2,0:T(8,128)(2,1)S(1)}, bf16[2,512,512]{1,2,0:T(8,128)(2,1)S(1)}, u32[]{:S(2)}, u32[]{:S(2)}) %collective-permute-start.2) | collective-permute-done | bytes 1048608 | tf_op jit(solution)/shard_map/ppermute | solution.py:26
  106.5 19.8 %collective-permute-done.3 = bf16[2,512,512]{1,2,0:T(8,128)(2,1)S(1)} collective-permute-done((bf16[2,512,512]{1,2,0:T(8,128)(2,1)S(1)}, bf16[2,512,512]{1,2,0:T(8,128)(2,1)S(1)}, u32[]{:S(2)}, u32[]{:S(2)}) %collective-permute-start.3) | collective-permute-done | bytes 1048608 | tf_op jit(solution)/shard_map/ppermute | solution.py:26
  126.4 27.4 %collective-permute-done.4 = bf16[2,512,512]{1,2,0:T(8,128)(2,1)S(1)} collective-permute-done((bf16[2,512,512]{1,2,0:T(8,128)(2,1)S(1)}, bf16[2,512,512]{1,2,0:T(8,128)(2,1)S(1)}, u32[]{:S(2)}, u32[]{:S(2)}) %collective-permute-start.4) | collective-permute-done | bytes 1048608 | tf_op jit(solution)/shard_map/ppermute | solution.py:26
  156.0 11.1 fusion
  167.1 11.9 exponential_reduce_fusion
  179.0 12.3 convolution_convert_fusion.3
  191.3 5.1 fusion.81
  196.5 2.7 convert_element_type.130
  202.2 159.8 %all-reduce.5.cloned.1.call-done = f32[512,2048]{1,0:T(8,128)} async-done(((f32[512,2048]{1,0:T(8,128)}), f32[512,2048]{1,0:T(8,128)}) %all-reduce.5.cloned.1.call-update) | async-done | bytes 4194320 | tf_op jit(solution)/shard_map/psum | solution.py:165
  362.0 3.4 fusion.75
  367.9 50.0 %all-gather.9.cloned.1.call-done = bf16[2048,2048]{1,0:T(8,128)(2,1)} async-done(((bf16[256,2048]{1,0:T(8,128)(2,1)}), bf16[2048,2048]{1,0:T(8,128)(2,1)}) %all-gather.9.cloned.1.call-update) | async-done | bytes 8388624 | tf_op jit(solution)/shard_map/all_gather | solution.py:128
  417.9 18.3 %fusion.19 = (bf16[512,2048]{1,0:T(8,128)(2,1)}, f32[512,2048]{1,0:T(8,128)}) fusion(bf16[2048,2048]{1,0:T(8,128)(2,1)} %all-gather.9.cloned.1.call-done, f32[512,2048]{1,0:T(8,128)} %copy-done.1, f32[2048]{0:T(1024)S(1)} %bitcast.102, f32[2048]{0:T(1024)S(1)} %bitcast.94, f32[512]{0:T(512)S(1)} %add_rsqrt_fusion, f32[512]{0:T(512)S(1)} %broadcast_multiply_fusion.4), kind=kOutput, calls=%fused_computation.42 | convolution fusion | flops 4368367616 | bytes 18894848 | tf_op jit(solution)/shard_map/dot_general | solution.py:169
  436.3 40.1 %all-gather.11.cloned.1.call-done = bf16[2048,2048]{1,0:T(8,128)(2,1)} async-done(((bf16[2048,256]{1,0:T(8,128)(2,1)}), bf16[2048,2048]{1,0:T(8,128)(2,1)}) %all-gather.11.cloned.1.call-update) | async-done | bytes 8388624 | tf_op jit(solution)/shard_map/all_gather | solution.py:129
  476.4 9.3 fusion.25
  487.0 6.1 fusion.82
  493.6 9.8 convolution_convert_fusion
  503.5 144.8 %all-reduce.9.cloned.1.call-done = f32[512,2048]{1,0:T(8,128)} async-done(((f32[512,2048]{1,0:T(8,128)}), f32[512,2048]{1,0:T(8,128)}) %all-reduce.9.cloned.1.call-update) | async-done | bytes 4194320 | tf_op jit(solution)/shard_map/psum | solution.py:179
  648.3 4.4 multiply_reduce_fusion.1
  652.7 84.1 %all-reduce.7.cloned.1.call-done = bf16[512,2048]{1,0:T(8,128)(2,1)} async-done(((bf16[512,2048]{1,0:T(8,128)(2,1)}), bf16[512,2048]{1,0:T(8,128)(2,1)}) %all-reduce.7.cloned.1.call-update) | async-done | bytes 2097168 | tf_op jit(solution)/shard_map/psum | solution.py:171
  736.8 7.0 multiply_add_fusion
  747.1 21.0 %multiply_reduce_fusion = (f32[4,512]{1,0:T(4,128)S(1)}, f32[4,512,3072]{2,1,0:T(8,128)}) fusion(f32[4,512,3072]{2,1,0:T(8,128)} %get-tuple-element.158, f32[4,512]{1,0:T(4,128)S(1)} %log_add_fusion, pred[512,3072]{1,0:T(8,128)(4,1)S(1)} %compare_and_fusion, bf16[512,4,128]{0,2,1:T(8,128)(2,1)S(1)} %bitcast.86, bf16[3072,4,128]{0,2,1:T(8,128)(2,1)} %bitcast.77), kind=kOutput, calls=%fused_computation.1 | convolution fusion | flops 1642067968 | bytes 55590912 | tf_op jit(solution)/shard_map/qhd,khd->hqk/dot_general | solution.py:190
  768.2 14.9 fusion.64
  783.0 17.2 %multiply_convert_fusion = bf16[4,512,3072]{2,1,0:T(8,128)(2,1)S(1)} fusion(f32[4,512,3072]{2,1,0:T(8,128)} %get-tuple-element.162, f32[4,512,3072]{2,1,0:T(8,128)} %get-tuple-element.158, f32[4,512]{1,0:T(4,128)S(1)} %get-tuple-element.161, f32[4,512]{1,0:T(4,128)S(1)} %log_add_fusion, pred[512,3072]{1,0:T(8,128)(4,1)S(1)} %compare_and_fusion), kind=kLoop, calls=%fused_computation | loop fusion | flops 37748736 | bytes 64503808 | tf_op jit(solution)/shard_map/convert_element_type | solution.py:192
  800.2 5.1 convolution_multiply_fusion
  806.7 6.5 copy.88
  813.2 6.6 copy.89
  819.8 7.5 fusion.43
  832.4 4.3 collective-permute-start.5
  836.8 8.9 fusion.49
  845.9 30.8 %collective-permute-done.9 = f32[2,512,512]{2,1,0:T(8,128)S(1)} collective-permute-done((f32[2,512,512]{2,1,0:T(8,128)}, f32[2,512,512]{2,1,0:T(8,128)S(1)}, u32[]{:S(2)}, u32[]{:S(2)}) %collective-permute-start.9) | collective-permute-done | bytes 2097184 | tf_op jit(solution)/shard_map/ppermute | solution.py:26
  876.7 3.9 collective-permute-done.7
  880.6 5.3 fusion.46
  886.9 7.7 convolution_bitcast_fusion.1
  895.6 5.4 fusion.50
  901.1 254.9 %all-reduce.11.cloned.1.call-done = f32[512,2048]{1,0:T(8,128)} async-done(((f32[512,2048]{1,0:T(8,128)}), f32[512,2048]{1,0:T(8,128)}) %all-reduce.11.cloned.1.call-update) | async-done | bytes 4194320 | tf_op jit(solution)/shard_map/psum | solution.py:212
  1156.0 3.9 fusion.15
  1162.8 8.5 convolution_bitcast_fusion
  1172.0 14.0 fusion.67
  1186.3 12.7 fusion.83
  1201.0 3.1 copy.93
  1204.1 3.0 copy.94
  1212.2 38.1 %reduce-scatter.19.cloned.1.call-done = f32[256,2]{1,0:T(8,128)} async-done(((f32[2048,2]{1,0:T(8,128)}), f32[256,2]{1,0:T(8,128)}) %reduce-scatter.19.cloned.1.call-update) | async-done | bytes 2064
  1251.3 39.2 %reduce-scatter.21.cloned.1.call-done = f32[256,2]{1,0:T(8,128)} async-done(((f32[2048,2]{1,0:T(8,128)}), f32[256,2]{1,0:T(8,128)}) %reduce-scatter.21.cloned.1.call-update) | async-done | bytes 2064
  1294.0 92.7 %reduce-scatter.11.cloned.1.call-done = f32[3,256,512]{1,2,0:T(8,128)} async-done(((f32[3,2048,512]{1,2,0:T(8,128)}), f32[3,256,512]{1,2,0:T(8,128)}) %reduce-scatter.11.cloned.1.call-update) | async-done | bytes 1572880 | tf_op jit(solution)/shard_map/reduce_scatter | solution.py:218
  1390.4 116.8 %reduce-scatter.15.cloned.1.call-done = f32[256,2048]{1,0:T(8,128)} async-done(((f32[2048,2048]{1,0:T(8,128)}), f32[256,2048]{1,0:T(8,128)}) %reduce-scatter.15.cloned.1.call-update) | async-done | bytes 2097168 | tf_op jit(solution)/shard_map/reduce_scatter | solution.py:220
  1507.2 2.7 multiply_reduce_fusion.7
  1510.6 117.0 %reduce-scatter.17.cloned.1.call-done = f32[2048,256]{1,0:T(8,128)} async-done(((f32[2048,2048]{1,0:T(8,128)}), f32[2048,256]{1,0:T(8,128)}) %reduce-scatter.17.cloned.1.call-update) | async-done | bytes 2097168 | tf_op jit(solution)/shard_map/reduce_scatter | solution.py:221
  1627.6 2.7 multiply_reduce_fusion.6
  1631.0 5.3 fusion.14
  1636.3 39.6 %psum.39 = f32[]{:T(128)} all-reduce(f32[]{:T(128)S(6)} %add.330), channel_id=1, replica_groups=mesh['ctx'=8,'tp'=4] {'ctx','tp'}, use_global_device_ids=true, to_apply=%region_36.37 | all-reduce | flops 1 | bytes 8 | tf_op jit(solution)/shard_map/psum | solution.py:229
  1676.6 5.7 add_multiply_fusion.2
  1682.4 3.1 copy.97
  1685.5 3.0 copy.98
  1693.0 3.0 add_multiply_fusion.3
  1696.1 7.0 add_multiply_fusion.1
  1703.0 3.6 add_multiply_fusion
  (196 shorter events, 49.9 us)
Async XLA Ops:
  7.2 5.7 copy-start.16
  7.2 6.5 copy-start.33
  7.2 16.9 copy-start.31
  7.2 25.8 %copy-start.2 = (bf16[512,2048]{1,0:T(8,128)(2,1)S(1)}, bf16[512,2048]{1,0:T(8,128)(2,1)}, u32[]{:S(2)}) copy-start(bf16[512,2048]{1,0:T(8,128)(2,1)} %param.22) | copy-start | bytes 6291460
  7.2 55.2 %all-gather.5.cloned.1.call-start = ((), (), s32[]{:S(2)}) async-start(), calls=%async_computation.6 | async-start | bytes 7077888 | tf_op jit(solution)/shard_map/all_gather | solution.py:126
  10.5 23.7 %copy-start.44 = (s32[4]{0:T(128)S(1)}, s32[4]{0:T(128)}, u32[]{:S(2)}) copy-start(s32[4]{0:T(128)} %param.42) | copy-start | bytes 52
  12.9 178.5 %all-gather.7.cloned.1.call-start = ((), (), s32[]{:S(2)}) async-start(), calls=%async_computation.7 | async-start | bytes 2359296 | tf_op jit(solution)/shard_map/all_gather | solution.py:127
  13.7 348.3 %all-reduce.5.cloned.1.call-start = ((), (), s32[]{:S(2)}) async-start(), calls=%async_computation.8 | async-start | bytes 8388608 | tf_op jit(solution)/shard_map/psum | solution.py:165
  24.1 44.9 %copy-start.37 = (f32[1,2048]{1,0:T(1,128)}, f32[1,2048]{1,0:T(1,128)S(1)}, u32[]{:S(2)}) copy-start(f32[1,2048]{1,0:T(1,128)S(1)} %get-tuple-element.150) | copy-start | bytes 24580
  24.2 393.8 %copy-start.35 = (f32[1,2048]{1,0:T(1,128)}, f32[1,2048]{1,0:T(1,128)S(1)}, u32[]{:S(2)}) copy-start(f32[1,2048]{1,0:T(1,128)S(1)} %get-tuple-element.149) | copy-start | bytes 24580
  33.1 36.0 %copy-start.22 = (f32[1,2048]{1,0:T(1,128)}, f32[1,2048]{1,0:T(1,128)S(1)}, u32[]{:S(2)}) copy-start(f32[1,2048]{1,0:T(1,128)S(1)} %get-tuple-element.148) | copy-start | bytes 24580
  33.5 35.6 %copy-start.24 = (f32[512]{0:T(512)}, f32[512]{0:T(512)S(1)}, u32[]{:S(2)}) copy-start(f32[512]{0:T(512)S(1)} %broadcast_multiply_fusion.5) | copy-start | bytes 6148
  34.2 34.9 %copy-start.26 = (f32[512]{0:T(512)}, f32[512]{0:T(512)S(1)}, u32[]{:S(2)}) copy-start(f32[512]{0:T(512)S(1)} %add_rsqrt_fusion.1) | copy-start | bytes 6148
  69.3 15.7 collective-permute-start
  70.7 14.5 collective-permute-start.1
  73.8 32.5 %collective-permute-start.2 = (bf16[2,512,512]{1,2,0:T(8,128)(2,1)S(1)}, bf16[2,512,512]{1,2,0:T(8,128)(2,1)S(1)}, u32[]{:S(2)}, u32[]{:S(2)}) collective-permute-start(bf16[2,512,512]{1,2,0:T(8,128)(2,1)S(1)} %get-tuple-element.145), channel_id=1, source_target_pairs={{0,8},{4,12},{8,16},{12,20},{16,24},{20,28},{1,9},{5,13},{9,17},{1... | collective-permute-start | bytes 3145736 | tf_op jit(solution)/shard_map/ppermute | solution.py:26
  77.2 49.0 %collective-permute-start.3 = (bf16[2,512,512]{1,2,0:T(8,128)(2,1)S(1)}, bf16[2,512,512]{1,2,0:T(8,128)(2,1)S(1)}, u32[]{:S(2)}, u32[]{:S(2)}) collective-permute-start(bf16[2,512,512]{1,2,0:T(8,128)(2,1)S(1)} %get-tuple-element.145), channel_id=1, source_target_pairs={{0,12},{4,16},{8,20},{12,24},{16,28},{1,13},{5,17},{9,21},{13,25},... | collective-permute-start | bytes 3145736 | tf_op jit(solution)/shard_map/ppermute | solution.py:26
  81.1 72.7 %collective-permute-start.4 = (bf16[2,512,512]{1,2,0:T(8,128)(2,1)S(1)}, bf16[2,512,512]{1,2,0:T(8,128)(2,1)S(1)}, u32[]{:S(2)}, u32[]{:S(2)}) collective-permute-start(bf16[2,512,512]{1,2,0:T(8,128)(2,1)S(1)} %get-tuple-element.145), channel_id=1, source_target_pairs={{0,16},{4,20},{8,24},{12,28},{1,17},{5,21},{9,25},{13,29},{2,18},{... | collective-permute-start | bytes 3145736 | tf_op jit(solution)/shard_map/ppermute | solution.py:26
  85.0 71.0 %copy-start.11 = (bf16[1,512,512]{1,2,0:T(8,128)(2,1)}, bf16[1,512,512]{1,2,0:T(8,128)(2,1)S(1)}, u32[]{:S(2)}) copy-start(bf16[1,512,512]{1,2,0:T(8,128)(2,1)S(1)} %slice.86) | copy-start | bytes 1572868
  156.0 11.1 copy-start.4
  191.3 5.2 copy-start.13
  196.5 221.5 %all-gather.9.cloned.1.call-start = ((), (), s32[]{:S(2)}) async-start(), calls=%async_computation.9 | async-start | bytes 9437184 | tf_op jit(solution)/shard_map/all_gather | solution.py:128
  199.3 277.1 %all-gather.11.cloned.1.call-start = ((), (), s32[]{:S(2)}) async-start(), calls=%async_computation.10 | async-start | bytes 9437184 | tf_op jit(solution)/shard_map/all_gather | solution.py:129
  202.0 446.3 %all-reduce.9.cloned.1.call-start = ((), (), s32[]{:S(2)}) async-start(), calls=%async_computation.12 | async-start | bytes 8388608 | tf_op jit(solution)/shard_map/psum | solution.py:179
  476.4 10.6 copy-start.43
  493.2 243.6 %all-reduce.7.cloned.1.call-start = ((), (), s32[]{:S(2)}) async-start(), calls=%async_computation.11 | async-start | bytes 4194304 | tf_op jit(solution)/shard_map/psum | solution.py:171
  503.5 652.6 %all-reduce.11.cloned.1.call-start = ((), (), s32[]{:S(2)}) async-start(), calls=%async_computation.13 | async-start | bytes 8388608 | tf_op jit(solution)/shard_map/psum | solution.py:212
  736.8 9.0 copy-start.15
  743.8 2.1 copy-start.6
  783.0 17.2 %copy-start.12 = (bf16[1,512,512]{1,2,0:T(8,128)(2,1)S(1)}, bf16[1,512,512]{1,2,0:T(8,128)(2,1)}, u32[]{:S(2)}) copy-start(bf16[1,512,512]{1,2,0:T(8,128)(2,1)} %copy-done.11) | copy-start | bytes 1572868
  800.2 6.5 copy-start
  819.8 17.0 copy-start.5
  827.2 49.5 %collective-permute-start.9 = (f32[2,512,512]{2,1,0:T(8,128)}, f32[2,512,512]{2,1,0:T(8,128)S(1)}, u32[]{:S(2)}, u32[]{:S(2)}) collective-permute-start(f32[2,512,512]{2,1,0:T(8,128)} %get-tuple-element.139), channel_id=1, source_target_pairs={{16,0},{20,4},{24,8},{28,12},{17,1},{21,5},{25,9},{29,13},{18,2},{... | collective-permute-start | bytes 6291464 | tf_op jit(solution)/shard_map/ppermute | solution.py:26
  828.5 48.2 %collective-permute-start.8 = (f32[2,512,512]{2,1,0:T(8,128)}, f32[2,512,512]{2,1,0:T(8,128)}, u32[]{:S(2)}, u32[]{:S(2)}) collective-permute-start(f32[2,512,512]{2,1,0:T(8,128)} %get-tuple-element.140), channel_id=1, source_target_pairs={{12,0},{16,4},{20,8},{24,12},{28,16},{13,1},{17,5},{21,9},{25,13},... | collective-permute-start | bytes 6291464 | tf_op jit(solution)/shard_map/ppermute | solution.py:26
  829.8 50.8 %collective-permute-start.7 = (f32[2,512,512]{2,1,0:T(8,128)}, f32[2,512,512]{2,1,0:T(8,128)}, u32[]{:S(2)}, u32[]{:S(2)}) collective-permute-start(f32[2,512,512]{2,1,0:T(8,128)} %get-tuple-element.138), channel_id=1, source_target_pairs={{8,0},{12,4},{16,8},{20,12},{24,16},{28,20},{9,1},{13,5},{17,9},{2... | collective-permute-start | bytes 6291464 | tf_op jit(solution)/shard_map/ppermute | solution.py:26
  831.1 49.5 %collective-permute-start.6 = (f32[2,512,512]{2,1,0:T(8,128)}, f32[2,512,512]{2,1,0:T(8,128)}, u32[]{:S(2)}, u32[]{:S(2)}) collective-permute-start(f32[2,512,512]{2,1,0:T(8,128)} %get-tuple-element.137), channel_id=1, source_target_pairs={{4,0},{8,4},{12,8},{16,12},{20,16},{24,20},{28,24},{5,1},{9,5},{13... | collective-permute-start | bytes 6291464 | tf_op jit(solution)/shard_map/ppermute | solution.py:26
  832.4 48.2 %collective-permute-start.5 = (f32[2,512,512]{2,1,0:T(8,128)}, f32[2,512,512]{2,1,0:T(8,128)}, u32[]{:S(2)}, u32[]{:S(2)}) collective-permute-start(f32[2,512,512]{2,1,0:T(8,128)} %get-tuple-element.136), channel_id=1, source_target_pairs={{0,4},{4,8},{8,12},{12,16},{16,20},{20,24},{24,28},{1,5},{5,9},{9,... | collective-permute-start | bytes 6291464 | tf_op jit(solution)/shard_map/ppermute | solution.py:26
  845.9 40.0 %copy-start.21 = (bf16[1,512,512]{2,1,0:T(8,128)(2,1)}, bf16[1,512,512]{2,1,0:T(8,128)(2,1)S(1)}, u32[]{:S(2)}) copy-start(bf16[1,512,512]{2,1,0:T(8,128)(2,1)S(1)} %copy.90) | copy-start | bytes 1572868
  894.6 315.8 %reduce-scatter.13.cloned.1.call-start = ((), (), s32[]{:S(2)}) async-start(), calls=%async_computation.15 | async-start | bytes 4718592 | tf_op jit(solution)/shard_map/reduce_scatter | solution.py:219
  901.0 255.0 %copy-start.3 = (bf16[512,2048]{1,0:T(8,128)(2,1)S(1)}, bf16[512,2048]{1,0:T(8,128)(2,1)}, u32[]{:S(2)}) copy-start(bf16[512,2048]{1,0:T(8,128)(2,1)} %param.22) | copy-start | bytes 6291460
  901.0 255.0 %copy-start.23 = (f32[1,2048]{1,0:T(1,128)S(1)}, f32[1,2048]{1,0:T(1,128)}, u32[]{:S(2)}) copy-start(f32[1,2048]{1,0:T(1,128)} %copy-done.22) | copy-start | bytes 24580
  901.0 255.0 %copy-start.25 = (f32[512]{0:T(512)S(1)}, f32[512]{0:T(512)}, u32[]{:S(2)}) copy-start(f32[512]{0:T(512)} %copy-done.24) | copy-start | bytes 6148
  901.0 255.0 %copy-start.27 = (f32[512]{0:T(512)S(1)}, f32[512]{0:T(512)}, u32[]{:S(2)}) copy-start(f32[512]{0:T(512)} %copy-done.26) | copy-start | bytes 6148
  901.1 261.7 %copy-start.20 = (bf16[2,512,512]{2,1,0:T(8,128)(2,1)S(1)}, bf16[2,512,512]{2,1,0:T(8,128)(2,1)}, u32[]{:S(2)}) copy-start(bf16[2,512,512]{2,1,0:T(8,128)(2,1)} %copy-done.19) | copy-start | bytes 3145732
  901.1 261.7 %copy-start.38 = (f32[1,2048]{1,0:T(1,128)S(1)}, f32[1,2048]{1,0:T(1,128)}, u32[]{:S(2)}) copy-start(f32[1,2048]{1,0:T(1,128)} %copy-done.37) | copy-start | bytes 24580
  901.1 349.2 %reduce-scatter.19.cloned.1.call-start = ((), (), s32[]{:S(2)}) async-start(), calls=%async_computation.18 | async-start | bytes 1179648
  1161.3 129.2 %reduce-scatter.21.cloned.1.call-start = ((), (), s32[]{:S(2)}) async-start(), calls=%async_computation.19 | async-start | bytes 1179648
  1162.7 223.9 %reduce-scatter.11.cloned.1.call-start = ((), (), s32[]{:S(2)}) async-start(), calls=%async_computation.14 | async-start | bytes 14155776 | tf_op jit(solution)/shard_map/reduce_scatter | solution.py:218
  1171.3 335.9 %reduce-scatter.15.cloned.1.call-start = ((), (), s32[]{:S(2)}) async-start(), calls=%async_computation.16 | async-start | bytes 18874368 | tf_op jit(solution)/shard_map/reduce_scatter | solution.py:220
  1186.0 441.6 %reduce-scatter.17.cloned.1.call-start = ((), (), s32[]{:S(2)}) async-start(), calls=%async_computation.17 | async-start | bytes 18874368 | tf_op jit(solution)/shard_map/reduce_scatter | solution.py:221
  1251.3 438.8 %copy-start.28 = (f32[2,256]{1,0:T(2,128)}, f32[2,256]{1,0:T(2,128)S(1)}, u32[]{:S(2)}) copy-start(f32[2,256]{1,0:T(2,128)S(1)} %copy.107) | copy-start | bytes 6148
  1291.5 399.3 %copy-start.29 = (f32[2,256]{1,0:T(2,128)}, f32[2,256]{1,0:T(2,128)S(1)}, u32[]{:S(2)}) copy-start(f32[2,256]{1,0:T(2,128)S(1)} %copy.109) | copy-start | bytes 6148
  1682.3 7.8 copy-start.32
  1682.3 7.8 copy-start.39
  1682.3 7.8 copy-start.40
  1682.3 8.4 copy-start.34
  1682.3 8.4 copy-start.41
  1682.3 8.4 copy-start.42
  1682.3 9.0 copy-start.7
  1693.0 3.0 copy-start.8
  1696.0 7.0 copy-start.9
  1696.0 7.0 copy-start.10
  1696.0 7.0 copy-start.17
  1696.1 7.0 copy-start.18
  (6 other events, 6.7 us)
Sparse Core Ops, SparseCore 0:
  13.0 49.4 all-gather.4
  64.9 37.4 all-gather.6
  196.6 165.3 all-reduce.4
  364.5 53.3 all-gather.8
  420.4 55.9 all-gather.10
  493.3 154.9 all-reduce.8
  651.2 85.5 all-reduce.6
  894.7 261.2 all-reduce.10
  1160.0 50.3 reduce-scatter.12
  1214.3 36.0 reduce-scatter.18
  1254.4 36.0 reduce-scatter.20
  1294.2 92.3 reduce-scatter.10
  1391.2 115.9 reduce-scatter.14
  1511.6 115.9 reduce-scatter.16
where the time goes:
time: 1720 us; the launch traced here: 1710 us
  waiting for transfers between devices  1270 us (74%)
  matrix products  178 us (10%)
  other arithmetic  110 us (6%)
  blocking collectives  58.8 us (3%)
  local copies, waits for them, and re-layouts  50.4 us (3%)
  between operations  24.9 us (1%)
  starting transfers between devices  24.5 us (1%)
    psum x1, waiting for transfers between devices, per_device(): grad_h1 = lax.psum(part_one, 'tp')  255 us
    psum x1, waiting for transfers between devices, per_device(): lax.psum(jnp.dot(attn_vals, out_full, preferred_element_type=jnp.float32)...  160 us
    psum x1, waiting for transfers between devices, per_device(): lax.psum(jnp.dot(grad_up_in, up_full.T, preferred_element_type=jnp.float3...  145 us
    reduce_scatter x1, waiting for transfers between devices, per_device(): lax.psum_scatter(grad_down, 'ctx', scatter_dimension=1, tiled=True)  117 us
    reduce_scatter x1, waiting for transfers between devices, per_device(): lax.psum_scatter(grad_up, 'ctx', scatter_dimension=0, tiled=True)  117 us
    ppermute x10, waiting for transfers between devices, passed_along(): lax.ppermute(value, axis, [(source, source + steps) for source in range(f...  103 us
    reduce_scatter x1, waiting for transfers between devices, per_device(): lax.psum_scatter(grad_qkvw, 'ctx', scatter_dimension=1, tiled=True)  92.7 us
    psum x1, waiting for transfers between devices, per_device(): lax.psum(jnp.dot(act_low, down_full, preferred_element_type=jnp.float32)....  84.1 us
  transfers between devices with their start and end apart: 24, of which 17 were waited for; matrix products, arithmetic and copies ran while one was open for 10% of the time, Pallas kernels for 0%

commit v1 on v0

--- a/solution.py
+++ b/solution.py
@@ -176,7 +176,10 @@
     grad_act = jnp.dot(cotangent, down_full.T, preferred_element_type=jnp.float32)
     grad_up_in = (grad_act * gelu_slope(up)).astype(jnp.bfloat16)
     grad_up = jnp.dot(a2.T, grad_up_in, preferred_element_type=jnp.float32)
-    grad_h2 = lax.psum(jnp.dot(grad_up_in, up_full.T, preferred_element_type=jnp.float32), "tp")
+    grad_h2 = jnp.sum(
+        lax.all_gather(jnp.dot(grad_up_in, up_full.T, preferred_element_type=jnp.float32), "tp"),
+        axis=0,
+    )
     grad_y1_norm, gain_two, bias_two = norm_back(grad_h2, normed2, rstd2, gains32[1])
     grad_y1 = cotangent.astype(jnp.float32) + grad_y1_norm
     grad_attn = grad_y1.astype(jnp.bfloat16)

time: 1720 us -> 1860 us (1.081)
  waiting for transfers between devices: 1270 us -> 1400 us
    all_gather x0 -> x1, waiting for transfers between devices: none -> 277 us  [per_device(): lax.all_gather(jnp.dot(grad_up_in, up_full.T, preferred_element_type=jnp....]
    psum x1 -> x0, waiting for transfers between devices: 145 us -> none  [per_device(): lax.psum(jnp.dot(grad_up_in, up_full.T, preferred_element_type=jnp.float3...]
    psum x1, waiting for transfers between devices: 255 us -> 166 us  [per_device(): grad_h1 = lax.psum(part_one, 'tp')]
    ppermute x10, waiting for transfers between devices: 103 us -> 169 us  [passed_along(): lax.ppermute(value, axis, [(source, source + steps) for source in range(f...]
    reduce_scatter x1, waiting for transfers between devices: 0.02 us -> 52.9 us  [per_device(): lax.psum_scatter(grad_outw, 'ctx', scatter_dimension=1, tiled=True)]
    reduce_scatter x1, waiting for transfers between devices: 117 us -> 91.9 us  [per_device(): lax.psum_scatter(grad_up, 'ctx', scatter_dimension=0, tiled=True)]
  transfers between devices with their start and end apart: 24 -> 24, of which waited for: 17 -> 18; matrix products, arithmetic and copies ran while one was open for 10% -> 10% of each run, Pallas kernels for 0% -> 0%
where the time goes in v1:
time: 1860 us; the launch traced here: 1850 us
  waiting for transfers between devices  1400 us (75%)
  matrix products  173 us (9%)
  other arithmetic  127 us (7%)
  blocking collectives  58.7 us (3%)
  local copies, waits for them, and re-layouts  53.4 us (3%)
  between operations  24.7 us (1%)
  starting transfers between devices  21.6 us (1%)
    all_gather x1, waiting for transfers between devices, per_device(): lax.all_gather(jnp.dot(grad_up_in, up_full.T, preferred_element_type=jnp....  277 us
    ppermute x10, waiting for transfers between devices, passed_along(): lax.ppermute(value, axis, [(source, source + steps) for source in range(f...  169 us
    psum x1, waiting for transfers between devices, per_device(): grad_h1 = lax.psum(part_one, 'tp')  166 us
    psum x1, waiting for transfers between devices, per_device(): lax.psum(jnp.dot(attn_vals, out_full, preferred_element_type=jnp.float32)...  162 us
    reduce_scatter x1, waiting for transfers between devices, per_device(): lax.psum_scatter(grad_down, 'ctx', scatter_dimension=1, tiled=True)  118 us
    reduce_scatter x1, waiting for transfers between devices, per_device(): lax.psum_scatter(grad_qkvw, 'ctx', scatter_dimension=1, tiled=True)  92.3 us
    reduce_scatter x1, waiting for transfers between devices, per_device(): lax.psum_scatter(grad_up, 'ctx', scatter_dimension=0, tiled=True)  91.9 us
    unnamed x16, waiting for transfers between devices  76.9 us
  transfers between devices with their start and end apart: 24, of which 18 were waited for; matrix products, arithmetic and copies ran while one was open for 10% of the time, Pallas kernels for 0%

profile of v1, /device:TPU:0, one launch (start us, length us, event | category | flops | bytes accessed | tf_op | source)
XLA Modules:
  0.0 1853.8 jit_solution(5474226827711080115)
XLA Ops:
  7.3 3.2 copy.83
  15.1 10.3 all_gather.25
  25.4 8.9 all_gather.24
  34.8 27.6 %all-gather.7.cloned.1.call-done = bf16[3,2048,512]{1,2,0:T(8,128)(2,1)} async-done(((bf16[3,256,512]{1,2,0:T(8,128)(2,1)}), bf16[3,2048,512]{1,2,0:T(8,128)(2,1)}) %all-gather.7.cloned.1.call-update) | async-done | bytes 6291472 | tf_op jit(solution)/shard_map/all_gather | solution.py:126
  62.4 6.6 fusion.48
  70.6 4.5 collective-permute-start.2
  76.9 3.0 collective-permute-start.4
  84.9 19.2 %collective-permute-done.2 = bf16[2,512,512]{1,2,0:T(8,128)(2,1)S(1)} collective-permute-done((bf16[2,512,512]{1,2,0:T(8,128)(2,1)S(1)}, bf16[2,512,512]{1,2,0:T(8,128)(2,1)S(1)}, u32[]{:S(2)}, u32[]{:S(2)}) %collective-permute-start.2) | collective-permute-done | bytes 1048608 | tf_op jit(solution)/shard_map/ppermute | solution.py:26
  104.3 21.8 %collective-permute-done.3 = bf16[2,512,512]{1,2,0:T(8,128)(2,1)S(1)} collective-permute-done((bf16[2,512,512]{1,2,0:T(8,128)(2,1)S(1)}, bf16[2,512,512]{1,2,0:T(8,128)(2,1)S(1)}, u32[]{:S(2)}, u32[]{:S(2)}) %collective-permute-start.3) | collective-permute-done | bytes 1048608 | tf_op jit(solution)/shard_map/ppermute | solution.py:26
  126.3 25.5 %collective-permute-done.4 = bf16[2,512,512]{1,2,0:T(8,128)(2,1)S(1)} collective-permute-done((bf16[2,512,512]{1,2,0:T(8,128)(2,1)S(1)}, bf16[2,512,512]{1,2,0:T(8,128)(2,1)S(1)}, u32[]{:S(2)}, u32[]{:S(2)}) %collective-permute-start.4) | collective-permute-done | bytes 1048608 | tf_op jit(solution)/shard_map/ppermute | solution.py:26
  154.1 11.1 fusion
  165.2 11.9 exponential_reduce_fusion
  177.0 12.3 convolution_convert_fusion.3
  189.4 5.1 fusion.81
  200.5 161.7 %all-reduce.4.cloned.1.call-done = f32[512,2048]{1,0:T(8,128)} async-done(((f32[512,2048]{1,0:T(8,128)}), f32[512,2048]{1,0:T(8,128)}) %all-reduce.4.cloned.1.call-update) | async-done | bytes 4194320 | tf_op jit(solution)/shard_map/psum | solution.py:165
  362.2 3.4 fusion.75
  368.2 49.9 %all-gather.11.cloned.1.call-done = bf16[2048,2048]{1,0:T(8,128)(2,1)} async-done(((bf16[256,2048]{1,0:T(8,128)(2,1)}), bf16[2048,2048]{1,0:T(8,128)(2,1)}) %all-gather.11.cloned.1.call-update) | async-done | bytes 8388624 | tf_op jit(solution)/shard_map/all_gather | solution.py:128
  418.1 18.3 fusion.19
  436.4 40.1 %all-gather.13.cloned.1.call-done = bf16[2048,2048]{1,0:T(8,128)(2,1)} async-done(((bf16[2048,256]{1,0:T(8,128)(2,1)}), bf16[2048,2048]{1,0:T(8,128)(2,1)}) %all-gather.13.cloned.1.call-update) | async-done | bytes 8388624 | tf_op jit(solution)/shard_map/all_gather | solution.py:129
  476.6 9.3 fusion.25
  487.2 6.1 fusion.82
  493.6 9.8 convolution_convert_fusion
  503.5 276.8 %all-gather.15.cloned.1.call-done = f32[2048,2048]{1,0:T(8,128)} async-done(((f32[512,2048]{1,0:T(8,128)}), f32[2048,2048]{1,0:T(8,128)}) %all-gather.15.cloned.1.call-update) | async-done | bytes 16777232 | tf_op jit(solution)/shard_map/all_gather | solution.py:180
  780.3 10.2 reduce_sum.234
  790.5 4.3 multiply_reduce_fusion.1
  794.8 73.3 %all-reduce.6.cloned.1.call-done = bf16[512,2048]{1,0:T(8,128)(2,1)} async-done(((bf16[512,2048]{1,0:T(8,128)(2,1)}), bf16[512,2048]{1,0:T(8,128)(2,1)}) %all-reduce.6.cloned.1.call-update) | async-done | bytes 2097168 | tf_op jit(solution)/shard_map/psum | solution.py:171
  868.1 6.9 multiply_add_fusion
  878.3 15.0 fusion.64
  893.3 21.0 %multiply_reduce_fusion = (f32[4,512]{1,0:T(4,128)S(1)}, f32[4,512,3072]{2,1,0:T(8,128)}) fusion(f32[4,512,3072]{2,1,0:T(8,128)} %get-tuple-element.157, f32[4,512]{1,0:T(4,128)S(1)} %log_add_fusion, pred[512,3072]{1,0:T(8,128)(4,1)S(1)} %compare_and_fusion, bf16[512,4,128]{0,2,1:T(8,128)(2,1)S(1)} %bitcast.89, bf16[3072,4,128]{0,2,1:T(8,128)(2,1)} %bitcast.79), kind=kOutput, calls=%fused_computation.1 | convolution fusion | flops 1642067968 | bytes 55590912 | tf_op jit(solution)/shard_map/qhd,khd->hqk/dot_general | solution.py:193
  914.4 6.6 copy.89
  920.9 17.4 multiply_convert_fusion
  938.4 5.2 convolution_multiply_fusion
  944.8 6.5 copy.88
  951.3 7.5 fusion.43
  965.9 8.9 fusion.49
  975.0 82.6 %collective-permute-done.7 = f32[2,512,512]{2,1,0:T(8,128)} collective-permute-done((f32[2,512,512]{2,1,0:T(8,128)}, f32[2,512,512]{2,1,0:T(8,128)}, u32[]{:S(2)}, u32[]{:S(2)}) %collective-permute-start.7) | collective-permute-done | bytes 2097184 | tf_op jit(solution)/shard_map/ppermute | solution.py:26
  1057.6 19.6 %collective-permute-done.8 = f32[2,512,512]{2,1,0:T(8,128)} collective-permute-done((f32[2,512,512]{2,1,0:T(8,128)}, f32[2,512,512]{2,1,0:T(8,128)}, u32[]{:S(2)}, u32[]{:S(2)}) %collective-permute-start.8) | collective-permute-done | bytes 2097184 | tf_op jit(solution)/shard_map/ppermute | solution.py:26
  1077.2 5.3 fusion.46
  1083.5 7.7 convolution_bitcast_fusion.1
  1092.8 10.6 fusion.67
  1105.0 9.7 fusion.83
  1115.8 5.5 fusion.50
  1121.4 6.7 reduce_sum.248
  1128.1 165.9 %all-reduce.8.cloned.1.call-done = f32[512,2048]{1,0:T(8,128)} async-done(((f32[512,2048]{1,0:T(8,128)}), f32[512,2048]{1,0:T(8,128)}) %all-reduce.8.cloned.1.call-update) | async-done | bytes 4194320 | tf_op jit(solution)/shard_map/psum | solution.py:215
  1294.1 3.6 fusion.15
  1300.6 9.3 convolution_bitcast_fusion
  1315.1 3.3 copy.93
  1318.4 3.3 copy.94
  1321.7 91.9 %reduce-scatter.15.cloned.1.call-done = f32[256,2048]{1,0:T(8,128)} async-done(((f32[2048,2048]{1,0:T(8,128)}), f32[256,2048]{1,0:T(8,128)}) %reduce-scatter.15.cloned.1.call-update) | async-done | bytes 2097168 | tf_op jit(solution)/shard_map/reduce_scatter | solution.py:223
  1413.6 2.7 multiply_reduce_fusion.7
  1416.4 117.7 %reduce-scatter.17.cloned.1.call-done = f32[2048,256]{1,0:T(8,128)} async-done(((f32[2048,2048]{1,0:T(8,128)}), f32[2048,256]{1,0:T(8,128)}) %reduce-scatter.17.cloned.1.call-update) | async-done | bytes 2097168 | tf_op jit(solution)/shard_map/reduce_scatter | solution.py:224
  1534.0 2.7 multiply_reduce_fusion.6
  1536.8 52.9 %reduce-scatter.13.cloned.1.call-done = f32[512,256]{1,0:T(8,128)} async-done(((f32[512,2048]{1,0:T(8,128)}), f32[512,256]{1,0:T(8,128)}) %reduce-scatter.13.cloned.1.call-update) | async-done | bytes 524304 | tf_op jit(solution)/shard_map/reduce_scatter | solution.py:222
  1591.5 37.9 %reduce-scatter.21.cloned.1.call-done = f32[256,2]{1,0:T(8,128)} async-done(((f32[2048,2]{1,0:T(8,128)}), f32[256,2]{1,0:T(8,128)}) %reduce-scatter.21.cloned.1.call-update) | async-done | bytes 2064
  1630.3 38.8 %reduce-scatter.19.cloned.1.call-done = f32[256,2]{1,0:T(8,128)} async-done(((f32[2048,2]{1,0:T(8,128)}), f32[256,2]{1,0:T(8,128)}) %reduce-scatter.19.cloned.1.call-update) | async-done | bytes 2064
  1672.6 92.3 %reduce-scatter.11.cloned.1.call-done = f32[3,256,512]{1,2,0:T(8,128)} async-done(((f32[3,2048,512]{1,2,0:T(8,128)}), f32[3,256,512]{1,2,0:T(8,128)}) %reduce-scatter.11.cloned.1.call-update) | async-done | bytes 1572880 | tf_op jit(solution)/shard_map/reduce_scatter | solution.py:221
  1769.9 5.3 fusion.14
  1775.2 39.5 %psum.31 = f32[]{:T(128)} all-reduce(f32[]{:T(128)S(6)} %add.328), channel_id=1, replica_groups=mesh['ctx'=8,'tp'=4] {'ctx','tp'}, use_global_device_ids=true, to_apply=%region_36.37 | all-reduce | flops 1 | bytes 8 | tf_op jit(solution)/shard_map/psum | solution.py:232
  1815.4 5.7 add_multiply_fusion.2
  1821.2 3.1 copy.97
  1824.3 3.0 copy.98
  1831.8 3.0 add_multiply_fusion.3
  1834.9 6.6 add_multiply_fusion
  1842.0 3.9 add_multiply_fusion.1
  (198 shorter events, 59.5 us)
Async XLA Ops:
  7.2 5.7 copy-start.16
  7.2 6.6 copy-start.43
  7.2 6.7 copy-start.34
  7.2 6.7 copy-start.32
  7.2 6.7 copy-start.2
  7.3 55.2 %all-gather.7.cloned.1.call-start = ((), (), s32[]{:S(2)}) async-start(), calls=%async_computation.6 | async-start | bytes 7077888 | tf_op jit(solution)/shard_map/all_gather | solution.py:126
  12.9 176.5 %all-gather.9.cloned.1.call-start = ((), (), s32[]{:S(2)}) async-start(), calls=%async_computation.7 | async-start | bytes 2359296 | tf_op jit(solution)/shard_map/all_gather | solution.py:127
  13.7 348.5 %all-reduce.4.cloned.1.call-start = ((), (), s32[]{:S(2)}) async-start(), calls=%async_computation.8 | async-start | bytes 8388608 | tf_op jit(solution)/shard_map/psum | solution.py:165
  14.4 54.6 %copy-start.25 = (f32[512]{0:T(512)}, f32[512]{0:T(512)S(1)}, u32[]{:S(2)}) copy-start(f32[512]{0:T(512)S(1)} %broadcast_multiply_fusion.5) | copy-start | bytes 6148
  15.1 53.9 %copy-start.27 = (f32[512]{0:T(512)}, f32[512]{0:T(512)S(1)}, u32[]{:S(2)}) copy-start(f32[512]{0:T(512)S(1)} %add_rsqrt_fusion.1) | copy-start | bytes 6148
  34.3 34.7 %copy-start.23 = (f32[1,2048]{1,0:T(1,128)}, f32[1,2048]{1,0:T(1,128)S(1)}, u32[]{:S(2)}) copy-start(f32[1,2048]{1,0:T(1,128)S(1)} %get-tuple-element.147) | copy-start | bytes 24580
  34.3 34.7 %copy-start.36 = (f32[1,2048]{1,0:T(1,128)}, f32[1,2048]{1,0:T(1,128)S(1)}, u32[]{:S(2)}) copy-start(f32[1,2048]{1,0:T(1,128)S(1)} %get-tuple-element.149) | copy-start | bytes 24580
  69.3 15.4 collective-permute-start
  70.6 33.5 %collective-permute-start.2 = (bf16[2,512,512]{1,2,0:T(8,128)(2,1)S(1)}, bf16[2,512,512]{1,2,0:T(8,128)(2,1)S(1)}, u32[]{:S(2)}, u32[]{:S(2)}) collective-permute-start(bf16[2,512,512]{1,2,0:T(8,128)(2,1)S(1)} %get-tuple-element.144), channel_id=1, source_target_pairs={{0,8},{4,12},{8,16},{12,20},{16,24},{20,28},{1,9},{5,13},{9,17},{1... | collective-permute-start | bytes 3145736 | tf_op jit(solution)/shard_map/ppermute | solution.py:26
  75.1 9.7 collective-permute-start.1
  76.9 74.9 %collective-permute-start.4 = (bf16[2,512,512]{1,2,0:T(8,128)(2,1)S(1)}, bf16[2,512,512]{1,2,0:T(8,128)(2,1)S(1)}, u32[]{:S(2)}, u32[]{:S(2)}) collective-permute-start(bf16[2,512,512]{1,2,0:T(8,128)(2,1)S(1)} %get-tuple-element.144), channel_id=1, source_target_pairs={{0,16},{4,20},{8,24},{12,28},{1,17},{5,21},{9,25},{13,29},{2,18},{... | collective-permute-start | bytes 3145736 | tf_op jit(solution)/shard_map/ppermute | solution.py:26
  79.9 46.3 %collective-permute-start.3 = (bf16[2,512,512]{1,2,0:T(8,128)(2,1)S(1)}, bf16[2,512,512]{1,2,0:T(8,128)(2,1)S(1)}, u32[]{:S(2)}, u32[]{:S(2)}) collective-permute-start(bf16[2,512,512]{1,2,0:T(8,128)(2,1)S(1)} %get-tuple-element.144), channel_id=1, source_target_pairs={{0,12},{4,16},{8,20},{12,24},{16,28},{1,13},{5,17},{9,21},{13,25},... | collective-permute-start | bytes 3145736 | tf_op jit(solution)/shard_map/ppermute | solution.py:26
  84.6 69.5 %copy-start.11 = (bf16[1,512,512]{1,2,0:T(8,128)(2,1)}, bf16[1,512,512]{1,2,0:T(8,128)(2,1)S(1)}, u32[]{:S(2)}) copy-start(bf16[1,512,512]{1,2,0:T(8,128)(2,1)S(1)} %slice.86) | copy-start | bytes 1572868
  154.1 11.1 copy-start.4
  189.3 5.2 copy-start.13
  194.5 223.6 %all-gather.11.cloned.1.call-start = ((), (), s32[]{:S(2)}) async-start(), calls=%async_computation.9 | async-start | bytes 9437184 | tf_op jit(solution)/shard_map/all_gather | solution.py:128
  197.3 279.3 %all-gather.13.cloned.1.call-start = ((), (), s32[]{:S(2)}) async-start(), calls=%async_computation.10 | async-start | bytes 9437184 | tf_op jit(solution)/shard_map/all_gather | solution.py:129
  200.0 580.3 %all-gather.15.cloned.1.call-start = ((), (), s32[]{:S(2)}) async-start(), calls=%async_computation.17 | async-start | bytes 20971520 | tf_op jit(solution)/shard_map/all_gather | solution.py:180
  365.5 2.1 copy-start.1
  476.6 10.6 copy-start.42
  493.4 374.7 %all-reduce.6.cloned.1.call-start = ((), (), s32[]{:S(2)}) async-start(), calls=%async_computation.11 | async-start | bytes 4194304 | tf_op jit(solution)/shard_map/psum | solution.py:171
  503.4 790.6 %all-reduce.8.cloned.1.call-start = ((), (), s32[]{:S(2)}) async-start(), calls=%async_computation.12 | async-start | bytes 8388608 | tf_op jit(solution)/shard_map/psum | solution.py:215
  868.1 9.0 copy-start.15
  875.0 2.0 copy-start.6
  920.9 17.4 copy-start.12
  938.4 6.4 copy-start
  951.3 14.6 copy-start.5
  958.8 16.2 collective-permute-start.5
  960.6 14.3 collective-permute-start.6
  961.9 95.6 %collective-permute-start.7 = (f32[2,512,512]{2,1,0:T(8,128)}, f32[2,512,512]{2,1,0:T(8,128)}, u32[]{:S(2)}, u32[]{:S(2)}) collective-permute-start(f32[2,512,512]{2,1,0:T(8,128)} %get-tuple-element.137), channel_id=1, source_target_pairs={{8,0},{12,4},{16,8},{20,12},{24,16},{28,20},{9,1},{13,5},{17,9},{2... | collective-permute-start | bytes 6291464 | tf_op jit(solution)/shard_map/ppermute | solution.py:26
  963.2 94.3 %collective-permute-start.9 = (f32[2,512,512]{2,1,0:T(8,128)}, f32[2,512,512]{2,1,0:T(8,128)}, u32[]{:S(2)}, u32[]{:S(2)}) collective-permute-start(f32[2,512,512]{2,1,0:T(8,128)} %get-tuple-element.138), channel_id=1, source_target_pairs={{16,0},{20,4},{24,8},{28,12},{17,1},{21,5},{25,9},{29,13},{18,2},{... | collective-permute-start | bytes 6291464 | tf_op jit(solution)/shard_map/ppermute | solution.py:26
  964.5 112.7 %collective-permute-start.8 = (f32[2,512,512]{2,1,0:T(8,128)}, f32[2,512,512]{2,1,0:T(8,128)}, u32[]{:S(2)}, u32[]{:S(2)}) collective-permute-start(f32[2,512,512]{2,1,0:T(8,128)} %get-tuple-element.139), channel_id=1, source_target_pairs={{12,0},{16,4},{20,8},{24,12},{28,16},{13,1},{17,5},{21,9},{25,13},... | collective-permute-start | bytes 6291464 | tf_op jit(solution)/shard_map/ppermute | solution.py:26
  975.0 107.5 %copy-start.22 = (bf16[1,512,512]{2,1,0:T(8,128)(2,1)}, bf16[1,512,512]{2,1,0:T(8,128)(2,1)S(1)}, u32[]{:S(2)}) copy-start(bf16[1,512,512]{2,1,0:T(8,128)(2,1)S(1)} %copy.90) | copy-start | bytes 1572868
  1091.2 322.4 %reduce-scatter.15.cloned.1.call-start = ((), (), s32[]{:S(2)}) async-start(), calls=%async_computation.15 | async-start | bytes 18874368 | tf_op jit(solution)/shard_map/reduce_scatter | solution.py:223
  1103.4 430.6 %reduce-scatter.17.cloned.1.call-start = ((), (), s32[]{:S(2)}) async-start(), calls=%async_computation.16 | async-start | bytes 18874368 | tf_op jit(solution)/shard_map/reduce_scatter | solution.py:224
  1114.7 474.9 %reduce-scatter.13.cloned.1.call-start = ((), (), s32[]{:S(2)}) async-start(), calls=%async_computation.14 | async-start | bytes 4718592 | tf_op jit(solution)/shard_map/reduce_scatter | solution.py:222
  1121.3 172.8 %copy-start.3 = (bf16[512,2048]{1,0:T(8,128)(2,1)S(1)}, bf16[512,2048]{1,0:T(8,128)(2,1)}, u32[]{:S(2)}) copy-start(bf16[512,2048]{1,0:T(8,128)(2,1)} %param.22) | copy-start | bytes 6291460
  1121.3 172.7 %copy-start.24 = (f32[1,2048]{1,0:T(1,128)S(1)}, f32[1,2048]{1,0:T(1,128)}, u32[]{:S(2)}) copy-start(f32[1,2048]{1,0:T(1,128)} %copy-done.23) | copy-start | bytes 24580
  1121.3 172.7 %copy-start.26 = (f32[512]{0:T(512)S(1)}, f32[512]{0:T(512)}, u32[]{:S(2)}) copy-start(f32[512]{0:T(512)} %copy-done.25) | copy-start | bytes 6148
  1121.3 172.7 %copy-start.28 = (f32[512]{0:T(512)S(1)}, f32[512]{0:T(512)}, u32[]{:S(2)}) copy-start(f32[512]{0:T(512)} %copy-done.27) | copy-start | bytes 6148
  1121.3 508.0 %reduce-scatter.21.cloned.1.call-start = ((), (), s32[]{:S(2)}) async-start(), calls=%async_computation.19 | async-start | bytes 1179648
  1128.1 172.5 %copy-start.21 = (bf16[2,512,512]{2,1,0:T(8,128)(2,1)S(1)}, bf16[2,512,512]{2,1,0:T(8,128)(2,1)}, u32[]{:S(2)}) copy-start(bf16[2,512,512]{2,1,0:T(8,128)(2,1)} %copy-done.20) | copy-start | bytes 3145732
  1128.1 172.5 %copy-start.37 = (f32[1,2048]{1,0:T(1,128)S(1)}, f32[1,2048]{1,0:T(1,128)}, u32[]{:S(2)}) copy-start(f32[1,2048]{1,0:T(1,128)} %copy-done.36) | copy-start | bytes 24580
  1299.1 370.0 %reduce-scatter.19.cloned.1.call-start = ((), (), s32[]{:S(2)}) async-start(), calls=%async_computation.18 | async-start | bytes 1179648
  1300.5 464.3 %reduce-scatter.11.cloned.1.call-start = ((), (), s32[]{:S(2)}) async-start(), calls=%async_computation.13 | async-start | bytes 14155776 | tf_op jit(solution)/shard_map/reduce_scatter | solution.py:221
  1630.3 198.7 %copy-start.29 = (f32[2,256]{1,0:T(2,128)}, f32[2,256]{1,0:T(2,128)S(1)}, u32[]{:S(2)}) copy-start(f32[2,256]{1,0:T(2,128)S(1)} %copy.109) | copy-start | bytes 6148
  1670.1 159.5 %copy-start.30 = (f32[2,256]{1,0:T(2,128)}, f32[2,256]{1,0:T(2,128)S(1)}, u32[]{:S(2)}) copy-start(f32[2,256]{1,0:T(2,128)S(1)} %copy.107) | copy-start | bytes 6148
  1821.1 7.8 copy-start.33
  1821.1 7.8 copy-start.38
  1821.1 7.8 copy-start.39
  1821.1 8.4 copy-start.35
  1821.1 8.4 copy-start.40
  1821.1 8.4 copy-start.41
  1821.1 9.0 copy-start.7
  1831.8 3.0 copy-start.8
  1834.8 6.7 copy-start.9
  1834.8 6.7 copy-start.10
  1834.8 6.7 copy-start.18
  1834.9 7.1 copy-start.19
  (6 other events, 7.2 us)
Sparse Core Ops, SparseCore 0:
  13.0 49.3 all-gather.6
  64.9 37.5 all-gather.8
  194.6 167.5 all-reduce.3
  364.7 53.3 all-gather.10
  420.6 55.9 all-gather.12
  493.5 286.7 all-gather.14
  783.3 84.6 all-reduce.5
  1091.3 202.6 all-reduce.7
  1298.6 114.9 reduce-scatter.14
  1418.0 115.9 reduce-scatter.16
  1538.3 51.2 reduce-scatter.12
  1593.3 35.9 reduce-scatter.20
  1633.1 35.9 reduce-scatter.18
  1672.4 92.3 reduce-scatter.10
